TPU v7x, 128 devices: a whole 4x4x4 slice. The times are simulated.
128 devices in a mesh: freq: 16 (over x, y), slab: 8 (over z, core).
Axes of the slice: x: 4, y: 4, z: 4, core: 2. Of those that a mesh axis runs over, the one named last changes fastest.
Arguments:
- fine_model: bfloat16 [2048, 2048], P(('freq', 'slab')), may hold values from 0.5 to 2
- resample: bfloat16 [16, 1024, 2048], P('freq', 'slab'), may hold values from -0.125 to 0.125
- lateral: bfloat16 [2048, 2048], replicated, may hold values from -0.0625 to 0.0625
- shift: float32 [16], P('freq'), may hold values from 0.5 to 4
- source: float32 [16, 1024, 2048], P('freq', 'slab'), may hold values from -6 to 6
- receiver: float32 [16, 1024, 2048], P('freq', 'slab'), may hold values from -6 to 6
Outputs:
- image: float32 [2048, 2048], P(('freq', 'slab'))
All inputs are finite; a program needn't handle non-finite values.
Results may differ from a plain program's by a relative error of at most 0.0029.
Values may be sent and summed in bfloat16 or wider, within the bound.
A program may use at most 128 MiB of HBM per device.

v0:
```python
import jax
import jax.numpy as jnp
from jax import lax
from jax.sharding import PartitionSpec as P

SWEEPS = 8
HALO = 8


def with_halo(value, size):
    up = [(i, i + 1) for i in range(size - 1)]
    down = [(i + 1, i) for i in range(size - 1)]
    before = lax.ppermute(value[-HALO:], "slab", up)
    after = lax.ppermute(value[:HALO], "slab", down)
    return jnp.concatenate([before, value, after], axis=0)


def shards(fine_model, resample, lateral, shift, source, receiver):
    freqs, slabs = (lax.axis_size("freq"), lax.axis_size("slab"))
    oper = resample[0]
    rows = oper.shape[0]
    every = lax.all_gather(oper, "slab", axis=0, tiled=True)
    wide = with_halo(oper, slabs)
    src = with_halo(source[0], slabs)
    model = lax.all_gather(fine_model, ("freq", "slab"), axis=0, tiled=True)
    coarse = jnp.dot(wide, model, preferred_element_type=jnp.float32)
    at = (
        lax.axis_index("slab") * rows
        - HALO
        + lax.broadcasted_iota(jnp.int32, (rows + 2 * HALO, 1), 0)
    )
    inside = (at >= 0) & (at < rows * slabs)
    inv = jnp.where(inside, 1.0 / (4.0 + shift[0] * coarse * coarse), 0.0)
    field = src * inv
    for sweep in range(1, SWEEPS):
        padded = jnp.pad(field, ((1, 1), (0, 0)))
        beside = padded[2:] + padded[:-2]
        side = jnp.dot(field.astype(jnp.bfloat16), lateral, preferred_element_type=jnp.float32)
        field = (src + 0.5 * beside + side) * inv
    part = (field[HALO:-HALO] * receiver[0]).astype(jnp.bfloat16)
    cols = lax.all_to_all(part, "slab", split_axis=1, concat_axis=0, tiled=True)
    term = lax.dot_general(
        every, cols, (((0,), (0,)), ((), ())), preferred_element_type=jnp.float32
    )
    mine = lax.psum_scatter(term, "freq", scatter_dimension=0, tiled=True)
    return lax.all_to_all(mine, "slab", split_axis=0, concat_axis=1, tiled=True)


def solution(mesh):
    in_specs = (
        P(("freq", "slab"), None),
        P("freq", "slab", None),
        P(),
        P("freq"),
        P("freq", "slab", None),
        P("freq", "slab", None),
    )
    out_specs = P(("freq", "slab"), None)
    return jax.shard_map(shards, mesh=mesh, in_specs=in_specs, out_specs=out_specs, check_vma=False)
```

profile of v0, /device:TPU:1, one launch (start us, length us, event | category | flops | bytes accessed | tf_op | source)
XLA Modules:
  0.0 218.3 jit_solution(8704276760987448156)
XLA Ops:
  6.5 0.7 all-gather.4.cloned.1.call-update
  7.3 0.0 all-gather.6.cloned.1.call-start
  7.3 0.9 slice_bitcast_fusion.1
  8.2 4.9 %collective-permute-start = (f32[8,2048]{1,0:T(8,128)S(1)}, f32[8,2048]{1,0:T(8,128)S(1)}, u32[]{:S(2)}, u32[]{:S(2)}) collective-permute-start(f32[8,2048]{1,0:T(8,128)S(1)} %get-tuple-element.9), channel_id=1, source_target_pairs={{0,1},{1,2},{2,3},{3,4},{4,5},{5,6},{6,7},{8,9},{9,10},{10,11},{11... | collective-permute-start | bytes 196616 | tf_op jit(solution)/shard_map/ppermute | solution.py:13
  13.1 1.9 collective-permute-start.1
  15.1 0.0 all-gather.6.cloned.1.call-update
  15.1 0.8 slice_bitcast_fusion.3
  15.9 3.6 %collective-permute-start.2 = (bf16[8,2048]{1,0:T(8,128)(2,1)S(1)}, bf16[8,2048]{1,0:T(8,128)(2,1)S(1)}, u32[]{:S(2)}, u32[]{:S(2)}) collective-permute-start(bf16[8,2048]{1,0:T(8,128)(2,1)S(1)} %get-tuple-element.11), channel_id=1, source_target_pairs={{0,1},{1,2},{2,3},{3,4},{4,5},{5,6},{6,7},{8,9},{9,10},{10,11},{11... | collective-permute-start | bytes 98312 | tf_op jit(solution)/shard_map/ppermute | solution.py:13
  19.5 1.9 collective-permute-start.3
  22.1 2.6 %collective-permute-done.3 = bf16[8,2048]{1,0:T(8,128)(2,1)S(1)} collective-permute-done((bf16[8,2048]{1,0:T(8,128)(2,1)S(1)}, bf16[8,2048]{1,0:T(8,128)(2,1)S(1)}, u32[]{:S(2)}, u32[]{:S(2)}) %collective-permute-start.3) | collective-permute-done | bytes 32800 | tf_op jit(solution)/shard_map/ppermute | solution.py:14
  24.7 59.4 %all-gather.4.cloned.1.call-done = bf16[2048,2048]{1,0:T(8,128)(2,1)} async-done(((bf16[16,2048]{1,0:T(8,128)(2,1)}), bf16[2048,2048]{1,0:T(8,128)(2,1)}) %all-gather.4.cloned.1.call-update) | async-done | bytes 8388624 | tf_op jit(solution)/shard_map/all_gather | solution.py:25
  84.1 5.5 %pad_maximum_fusion = (f32[144,2048]{1,0:T(8,128)S(1)}, f32[144,2048]{1,0:T(8,128)S(1)}, f32[144,2048]{1,0:T(8,128)S(1)}) fusion(f32[8,2048]{1,0:T(8,128)S(1)} %collective-permute-done.1, f32[128,2048]{1,0:T(8,128)} %bitcast.43, f32[8,2048]{1,0:T(8,128)S(1)} %collective-permute-done, bf16[2048,2048]{1,0:T(8,128)(2,1)} %all-gather.4.cloned.1.call-done, ...), kind=kOutput, calls=%fused_computation.51 | convolution fusion | flops 1212088320 | bytes 13697172 | tf_op jit(solution)/shard_map/dot_general | solution.py:26
  89.6 0.8 slice-done.1
  90.4 0.2 copy-done
  90.7 1.6 fusion.9
  92.3 1.6 fusion.14
  93.9 1.6 fusion.19
  95.5 1.6 fusion.24
  97.1 1.6 fusion.29
  98.7 1.6 fusion.34
  100.3 0.4 pad_slice_fusion.1
  100.7 1.4 fusion.49
  102.1 0.6 fusion.39
  102.7 0.8 copy.16
  103.5 3.7 %all-to-all-start = ((bf16[128,8,256]{2,0,1:T(8,128)(2,1)}), bf16[128,8,256]{2,0,1:T(8,128)(2,1)S(1)}, u32[]{:S(2)}, u32[]{:S(2)}) async-start(bf16[128,8,256]{2,0,1:T(8,128)(2,1)} %bitcast.39), calls=%async_computation | async-start | bytes 1048576 | tf_op jit(solution)/shard_map/all_to_all | solution.py:41
  107.2 12.3 %all-gather.6.cloned.1.call-done = bf16[1,1024,2048]{2,1,0:T(8,128)(2,1)} async-done(((bf16[1,128,2048]{2,1,0:T(8,128)(2,1)}), bf16[1,1024,2048]{2,1,0:T(8,128)(2,1)}) %all-gather.6.cloned.1.call-update) | async-done | bytes 4194320 | tf_op jit(solution)/shard_map/all_gather | solution.py:22
  119.4 0.1 all-to-all-done
  119.6 4.8 %fusion.2 = f32[2048,256]{0,1:T(8,128)} fusion(bf16[1024,256]{1,0:T(8,128)(2,1)S(1)} %bitcast.52, bf16[1,1024,2048]{2,1,0:T(8,128)(2,1)} %all-gather.6.cloned.1.call-done), kind=kOutput, calls=%fused_computation.2 | convolution fusion | flops 1073741824 | bytes 6815744 | tf_op jit(solution)/shard_map/dot_general | solution.py:42
  124.4 73.9 %reduce-scatter.2.cloned.1.call-done = f32[128,256]{0,1:T(8,128)} async-done(((f32[2048,256]{0,1:T(8,128)}), f32[128,256]{0,1:T(8,128)}) %reduce-scatter.2.cloned.1.call-update) | async-done | bytes 131088 | tf_op jit(solution)/shard_map/reduce_scatter | solution.py:45
  198.3 1.0 copy.11
  199.3 11.9 %all_to_all.38 = f32[8,16,256]{2,1,0:T(8,128)S(1)} all-to-all(f32[8,16,256]{2,1,0:T(8,128)S(1)} %bitcast.53), channel_id=1, replica_groups=mesh['freq'=16,'slab'=8] {'slab'}, dimensions={0} | all-to-all | bytes 262144 | tf_op jit(solution)/shard_map/all_to_all | solution.py:46
  211.1 0.7 copy.14
  (14 shorter events, 0.0 us)
Async XLA Ops:
  6.5 77.6 %all-gather.4.cloned.1.call-start = ((), (), s32[]{:S(2)}) async-start(), calls=%async_computation.3 | async-start | bytes 8454144 | tf_op jit(solution)/shard_map/all_gather | solution.py:25
  7.3 112.2 %all-gather.6.cloned.1.call-start = ((), (), s32[]{:S(2)}) async-start(), calls=%async_computation.5 | async-start | bytes 4718592 | tf_op jit(solution)/shard_map/all_gather | solution.py:22
  8.2 16.6 %collective-permute-start = (f32[8,2048]{1,0:T(8,128)S(1)}, f32[8,2048]{1,0:T(8,128)S(1)}, u32[]{:S(2)}, u32[]{:S(2)}) collective-permute-start(f32[8,2048]{1,0:T(8,128)S(1)} %get-tuple-element.9), channel_id=1, source_target_pairs={{0,1},{1,2},{2,3},{3,4},{4,5},{5,6},{6,7},{8,9},{9,10},{10,11},{11... | collective-permute-start | bytes 196616 | tf_op jit(solution)/shard_map/ppermute | solution.py:13
  13.1 11.6 %collective-permute-start.1 = (f32[8,2048]{1,0:T(8,128)S(1)}, f32[8,2048]{1,0:T(8,128)S(1)}, u32[]{:S(2)}, u32[]{:S(2)}) collective-permute-start(f32[8,2048]{1,0:T(8,128)S(1)} %get-tuple-element.10), channel_id=1, source_target_pairs={{1,0},{2,1},{3,2},{4,3},{5,4},{6,5},{7,6},{9,8},{10,9},{11,10},{12... | collective-permute-start | bytes 196616 | tf_op jit(solution)/shard_map/ppermute | solution.py:14
  15.9 6.2 %collective-permute-start.2 = (bf16[8,2048]{1,0:T(8,128)(2,1)S(1)}, bf16[8,2048]{1,0:T(8,128)(2,1)S(1)}, u32[]{:S(2)}, u32[]{:S(2)}) collective-permute-start(bf16[8,2048]{1,0:T(8,128)(2,1)S(1)} %get-tuple-element.11), channel_id=1, source_target_pairs={{0,1},{1,2},{2,3},{3,4},{4,5},{5,6},{6,7},{8,9},{9,10},{10,11},{11... | collective-permute-start | bytes 98312 | tf_op jit(solution)/shard_map/ppermute | solution.py:13
  19.5 5.2 %collective-permute-start.3 = (bf16[8,2048]{1,0:T(8,128)(2,1)S(1)}, bf16[8,2048]{1,0:T(8,128)(2,1)S(1)}, u32[]{:S(2)}, u32[]{:S(2)}) collective-permute-start(bf16[8,2048]{1,0:T(8,128)(2,1)S(1)} %get-tuple-element.12), channel_id=1, source_target_pairs={{1,0},{2,1},{3,2},{4,3},{5,4},{6,5},{7,6},{9,8},{10,9},{11,10},{12... | collective-permute-start | bytes 98312 | tf_op jit(solution)/shard_map/ppermute | solution.py:14
  84.1 5.5 %slice-start = ((s8[8388608]{0:T(1024)(128)(4,1)}), s8[4194304]{0:T(1024)(128)(4,1)S(1)}, s32[]{:S(2)}) async-start(s8[8388608]{0:T(1024)(128)(4,1)} %bitcast.41), calls=%async_computation.6 | async-start | bytes 8388608
  84.1 6.3 %slice-start.1 = ((s8[8388608]{0:T(1024)(128)(4,1)}), s8[4194304]{0:T(1024)(128)(4,1)S(1)}, s32[]{:S(2)}) async-start(s8[8388608]{0:T(1024)(128)(4,1)} %bitcast.41), calls=%async_computation.7 | async-start | bytes 8388608
  84.1 6.5 %copy-start = (f32[1,128,2048]{2,1,0:T(8,128)S(1)}, f32[1,128,2048]{2,1,0:T(8,128)}, u32[]{:S(2)}) copy-start(f32[1,128,2048]{2,1,0:T(8,128)} %param.10) | copy-start | bytes 3145732
  100.6 1.4 copy-start.1
  103.5 16.1 %all-to-all-start = ((bf16[128,8,256]{2,0,1:T(8,128)(2,1)}), bf16[128,8,256]{2,0,1:T(8,128)(2,1)S(1)}, u32[]{:S(2)}, u32[]{:S(2)}) async-start(bf16[128,8,256]{2,0,1:T(8,128)(2,1)} %bitcast.39), calls=%async_computation | async-start | bytes 1048576 | tf_op jit(solution)/shard_map/all_to_all | solution.py:41
  107.2 91.1 %reduce-scatter.2.cloned.1.call-start = ((), (), s32[]{:S(2)}) async-start(), calls=%async_computation.4 | async-start | bytes 2228224 | tf_op jit(solution)/shard_map/reduce_scatter | solution.py:45
Sparse Core Ops, SparseCore 0:
  10.3 73.7 all-gather.3
  85.8 33.5 all-gather.5
  124.5 73.7 reduce-scatter.1
where the time goes:
time: 219 us; the launch traced here: 218 us
  waiting for transfers between devices  149 us (68%)
  matrix products  21.2 us (10%)
  starting transfers between devices  16.1 us (7%)
  between operations  13.9 us (6%)
  blocking collectives  11.9 us (5%)
  local copies, waits for them, and re-layouts  5.6 us (3%)
    reduce_scatter x1, waiting for transfers between devices, shards(): mine = lax.psum_scatter(term, 'freq', scatter_dimension=0, tiled=True)  73.9 us
    all_gather x1, waiting for transfers between devices, shards(): model = lax.all_gather(fine_model, ('freq', 'slab'), axis=0, tiled=True)  59.4 us
    all_gather x1, waiting for transfers between devices, shards(): every = lax.all_gather(oper, 'slab', axis=0, tiled=True)  12.3 us
    all_to_all x1, blocking collectives, shards(): return lax.all_to_all(mine, 'slab', split_axis=0, concat_axis=1, tiled=True)  11.9 us
    dot_general x7, matrix products, shards(): jnp.dot(field.astype(jnp.bfloat16), lateral, preferred_element_type=jnp.f...  10.9 us
    ppermute x2, starting transfers between devices, with_halo(): before = lax.ppermute(value[-HALO:], 'slab', up)  8.57 us
    dot_general x1, matrix products, shards(): coarse = jnp.dot(wide, model, preferred_element_type=jnp.float32)  5.46 us
    dot_general x1, matrix products, shards(): lax.dot_general(every, cols, (((0,), (0,)), ((), ())), preferred_element_...  4.78 us
  transfers between devices with their start and end apart: 8, of which 5 were waited for; matrix products, arithmetic and copies ran while one was open for 9% of the time, Pallas kernels for 0%

commit v1 on v0

--- a/solution.py
+++ b/solution.py
@@ -22,7 +22,10 @@
     every = lax.all_gather(oper, "slab", axis=0, tiled=True)
     wide = with_halo(oper, slabs)
     src = with_halo(source[0], slabs)
-    model = lax.all_gather(fine_model, ("freq", "slab"), axis=0, tiled=True)
+    count = lax.axis_size(("freq", "slab"))
+    shards_2 = jnp.stack([fine_model for _ in range(count)])
+    shards_2 = lax.all_to_all(shards_2, ("freq", "slab"), split_axis=0, concat_axis=0)
+    model = jnp.concatenate(shards_2, axis=0)
     coarse = jnp.dot(wide, model, preferred_element_type=jnp.float32)
     at = (
         lax.axis_index("slab") * rows

time: 219 us -> 259 us (1.18)
  waiting for transfers between devices: 149 us -> 171 us
  starting transfers between devices: 16.1 us -> 30.7 us
  local copies, waits for them, and re-layouts: 5.6 us -> 8.87 us
    ppermute x2, waiting for transfers between devices: 2.63 us -> 89.3 us  [with_halo(): after = lax.ppermute(value[:HALO], 'slab', down)]
    all_gather x1 -> x0, waiting for transfers between devices: 59.4 us -> none  [shards(): model = lax.all_gather(fine_model, ('freq', 'slab'), axis=0, tiled=True)]
    all_gather x1, waiting for transfers between devices: 12.3 us -> 0.01 us  [shards(): every = lax.all_gather(oper, 'slab', axis=0, tiled=True)]
    all_to_all x0 -> x1, starting transfers between devices: none -> 12 us  [shards(): lax.all_to_all(shards_2, ('freq', 'slab'), split_axis=0, concat_axis=0)]
    all_to_all x1, waiting for transfers between devices: 0.14 us -> 9.48 us  [shards(): cols = lax.all_to_all(part, 'slab', split_axis=1, concat_axis=0, tiled=True)]
    another operation x0 -> x1, local copies, waits for them, and re-layouts: none -> 5.12 us  [shards(): shards_2 = jnp.stack([fine_model for _ in range(count)])]
    all_to_all x1, starting transfers between devices: 3.65 us -> 7.52 us  [shards(): cols = lax.all_to_all(part, 'slab', split_axis=1, concat_axis=0, tiled=True)]
    reduce_scatter x1, waiting for transfers between devices: 73.9 us -> 70.9 us  [shards(): mine = lax.psum_scatter(term, 'freq', scatter_dimension=0, tiled=True)]
  transfers between devices with their start and end apart: 8 -> 8, of which waited for: 5 -> 4; matrix products, arithmetic and copies ran while one was open for 9% -> 7% of each run, Pallas kernels for 0% -> 0%
where the time goes in v1:
time: 259 us; the launch traced here: 258 us
  waiting for transfers between devices  171 us (66%)
  starting transfers between devices  30.7 us (12%)
  matrix products  20.9 us (8%)
  between operations  14.2 us (5%)
  blocking collectives  11.8 us (5%)
  local copies, waits for them, and re-layouts  8.87 us (3%)
    ppermute x2, waiting for transfers between devices, with_halo(): after = lax.ppermute(value[:HALO], 'slab', down)  89.3 us
    reduce_scatter x1, waiting for transfers between devices, shards(): mine = lax.psum_scatter(term, 'freq', scatter_dimension=0, tiled=True)  70.9 us
    all_to_all x1, starting transfers between devices, shards(): lax.all_to_all(shards_2, ('freq', 'slab'), split_axis=0, concat_axis=0)  12 us
    all_to_all x1, blocking collectives, shards(): return lax.all_to_all(mine, 'slab', split_axis=0, concat_axis=1, tiled=True)  11.8 us
    dot_general x7, matrix products, shards(): jnp.dot(field.astype(jnp.bfloat16), lateral, preferred_element_type=jnp.f...  10.9 us
    all_to_all x1, waiting for transfers between devices, shards(): cols = lax.all_to_all(part, 'slab', split_axis=1, concat_axis=0, tiled=True)  9.48 us
    all_to_all x1, starting transfers between devices, shards(): cols = lax.all_to_all(part, 'slab', split_axis=1, concat_axis=0, tiled=True)  7.52 us
    ppermute x2, starting transfers between devices, with_halo(): before = lax.ppermute(value[-HALO:], 'slab', up)  6.17 us
  transfers between devices with their start and end apart: 8, of which 4 were waited for; matrix products, arithmetic and copies ran while one was open for 7% of the time, Pallas kernels for 0%

profile of v1, /device:TPU:1, one launch (start us, length us, event | category | flops | bytes accessed | tf_op | source)
XLA Modules:
  0.0 258.2 jit_solution(5672706888894112103)
XLA Ops:
  6.5 5.1 %stack.2 = bf16[128,16,2048]{2,1,0:T(8,128)(2,1)} broadcast(bf16[16,2048]{1,0:T(8,128)(2,1)} %param.6), dimensions={1,2} | broadcast | bytes 8454144 | tf_op jit(solution)/shard_map/stack | solution.py:26
  11.7 12.0 %all-to-all-start = ((bf16[128,16,2048]{2,1,0:T(8,128)(2,1)}), bf16[128,16,2048]{2,1,0:T(8,128)(2,1)}, u32[]{:S(2)}, u32[]{:S(2)}) async-start(bf16[128,16,2048]{2,1,0:T(8,128)(2,1)} %stack.2), calls=%async_computation | async-start | bytes 16777216 | tf_op jit(solution)/shard_map/all_to_all | solution.py:27
  23.6 0.0 all-gather.3.cloned.1.call-start
  23.7 3.0 %collective-permute-start.1 = (f32[8,2048]{1,0:T(8,128)S(1)}, f32[8,2048]{1,0:T(8,128)S(1)}, u32[]{:S(2)}, u32[]{:S(2)}) collective-permute-start(f32[8,2048]{1,0:T(8,128)S(1)} %get-tuple-element.10), channel_id=1, source_target_pairs={{1,0},{2,1},{3,2},{4,3},{5,4},{6,5},{7,6},{9,8},{10,9},{11,10},{12... | collective-permute-start | bytes 196616 | tf_op jit(solution)/shard_map/ppermute | solution.py:14
  26.8 2.5 collective-permute-start
  29.3 0.0 all-gather.3.cloned.1.call-update
  29.3 1.9 collective-permute-start.3
  31.3 3.6 %collective-permute-start.2 = (bf16[8,2048]{1,0:T(8,128)(2,1)S(1)}, bf16[8,2048]{1,0:T(8,128)(2,1)S(1)}, u32[]{:S(2)}, u32[]{:S(2)}) collective-permute-start(bf16[8,2048]{1,0:T(8,128)(2,1)S(1)} %get-tuple-element.11), channel_id=1, source_target_pairs={{0,1},{1,2},{2,3},{3,4},{4,5},{5,6},{6,7},{8,9},{9,10},{10,11},{11... | collective-permute-start | bytes 98312 | tf_op jit(solution)/shard_map/ppermute | solution.py:13
  35.6 89.3 %collective-permute-done.3 = bf16[8,2048]{1,0:T(8,128)(2,1)S(1)} collective-permute-done((bf16[8,2048]{1,0:T(8,128)(2,1)S(1)}, bf16[8,2048]{1,0:T(8,128)(2,1)S(1)}, u32[]{:S(2)}, u32[]{:S(2)}) %collective-permute-start.3) | collective-permute-done | bytes 32800 | tf_op jit(solution)/shard_map/ppermute | solution.py:14
  124.9 0.0 collective-permute-done.1
  124.9 1.3 all-to-all-done
  126.2 5.2 %pad_maximum_fusion = (f32[144,2048]{1,0:T(8,128)S(1)}, f32[144,2048]{1,0:T(8,128)S(1)}, f32[144,2048]{1,0:T(8,128)S(1)}) fusion(f32[8,2048]{1,0:T(8,128)S(1)} %collective-permute-done.1, f32[128,2048]{1,0:T(8,128)S(1)} %bitcast.44, f32[8,2048]{1,0:T(8,128)S(1)} %collective-permute-done, bf16[2048,2048]{1,0:T(8,128)(2,1)} %bitcast.7, ...), kind=kOutput, calls=%fused_computation.51 | convolution fusion | flops 1212088320 | bytes 13697172 | tf_op jit(solution)/shard_map/dot_general | solution.py:29
  131.4 0.8 slice-done.1
  132.2 1.6 fusion.9
  133.8 1.6 fusion.14
  135.4 1.6 fusion.19
  137.0 1.6 fusion.24
  138.6 1.6 fusion.29
  140.2 1.6 fusion.34
  141.8 0.4 pad_slice_fusion.1
  142.2 0.0 copy-start.1
  142.2 1.4 fusion.49
  143.6 0.6 fusion.39
  144.3 0.8 copy.16
  145.1 7.5 %all-to-all-start.1 = ((bf16[128,8,256]{2,0,1:T(8,128)(2,1)}), bf16[128,8,256]{2,0,1:T(8,128)(2,1)S(1)}, u32[]{:S(2)}, u32[]{:S(2)}) async-start(bf16[128,8,256]{2,0,1:T(8,128)(2,1)} %bitcast.40), calls=%async_computation.1 | async-start | bytes 1048576 | tf_op jit(solution)/shard_map/all_to_all | solution.py:44
  152.6 9.5 %all-to-all-done.1 = bf16[128,8,256]{2,0,1:T(8,128)(2,1)S(1)} async-done(((bf16[128,8,256]{2,0,1:T(8,128)(2,1)}), bf16[128,8,256]{2,0,1:T(8,128)(2,1)S(1)}, u32[]{:S(2)}, u32[]{:S(2)}) %all-to-all-start.1) | async-done | bytes 524320 | tf_op jit(solution)/shard_map/all_to_all | solution.py:44
  162.1 4.8 %fusion.2 = f32[2048,256]{0,1:T(8,128)} fusion(bf16[1024,256]{1,0:T(8,128)(2,1)S(1)} %bitcast.53, bf16[1,1024,2048]{2,1,0:T(8,128)(2,1)} %all-gather.3.cloned.1.call-done), kind=kOutput, calls=%fused_computation.2 | convolution fusion | flops 1073741824 | bytes 6815744 | tf_op jit(solution)/shard_map/dot_general | solution.py:45
  166.9 0.0 reduce-scatter.2.cloned.1.call-update
  166.9 70.9 %reduce-scatter.2.cloned.1.call-done = f32[128,256]{0,1:T(8,128)} async-done(((f32[2048,256]{0,1:T(8,128)}), f32[128,256]{0,1:T(8,128)}) %reduce-scatter.2.cloned.1.call-update) | async-done | bytes 131088 | tf_op jit(solution)/shard_map/reduce_scatter | solution.py:48
  237.9 1.0 copy.11
  238.9 11.8 %all_to_all.43 = f32[8,16,256]{2,1,0:T(8,128)S(1)} all-to-all(f32[8,16,256]{2,1,0:T(8,128)S(1)} %bitcast.54), channel_id=1, replica_groups=mesh['freq'=16,'slab'=8] {'slab'}, dimensions={0} | all-to-all | bytes 262144 | tf_op jit(solution)/shard_map/all_to_all | solution.py:49
  250.7 0.7 copy.14
  (16 shorter events, 0.0 us)
Async XLA Ops:
  11.7 12.0 %copy-start = (f32[1,128,2048]{2,1,0:T(8,128)S(1)}, f32[1,128,2048]{2,1,0:T(8,128)}, u32[]{:S(2)}) copy-start(f32[1,128,2048]{2,1,0:T(8,128)} %param.10) | copy-start | bytes 3145732
  11.7 17.7 %copy-start.2 = (bf16[1,128,2048]{2,1,0:T(8,128)(2,1)S(1)}, bf16[1,128,2048]{2,1,0:T(8,128)(2,1)}, u32[]{:S(2)}) copy-start(bf16[1,128,2048]{2,1,0:T(8,128)(2,1)} %param.7) | copy-start | bytes 1572868
  11.7 114.6 %all-to-all-start = ((bf16[128,16,2048]{2,1,0:T(8,128)(2,1)}), bf16[128,16,2048]{2,1,0:T(8,128)(2,1)}, u32[]{:S(2)}, u32[]{:S(2)}) async-start(bf16[128,16,2048]{2,1,0:T(8,128)(2,1)} %stack.2), calls=%async_computation | async-start | bytes 16777216 | tf_op jit(solution)/shard_map/all_to_all | solution.py:27
  23.6 129.0 %all-gather.3.cloned.1.call-start = ((), (), s32[]{:S(2)}) async-start(), calls=%async_computation.5 | async-start | bytes 4718592 | tf_op jit(solution)/shard_map/all_gather | solution.py:22
  23.7 101.2 %collective-permute-start.1 = (f32[8,2048]{1,0:T(8,128)S(1)}, f32[8,2048]{1,0:T(8,128)S(1)}, u32[]{:S(2)}, u32[]{:S(2)}) collective-permute-start(f32[8,2048]{1,0:T(8,128)S(1)} %get-tuple-element.10), channel_id=1, source_target_pairs={{1,0},{2,1},{3,2},{4,3},{5,4},{6,5},{7,6},{9,8},{10,9},{11,10},{12... | collective-permute-start | bytes 196616 | tf_op jit(solution)/shard_map/ppermute | solution.py:14
  26.8 98.1 %collective-permute-start = (f32[8,2048]{1,0:T(8,128)S(1)}, f32[8,2048]{1,0:T(8,128)S(1)}, u32[]{:S(2)}, u32[]{:S(2)}) collective-permute-start(f32[8,2048]{1,0:T(8,128)S(1)} %get-tuple-element.9), channel_id=1, source_target_pairs={{0,1},{1,2},{2,3},{3,4},{4,5},{5,6},{6,7},{8,9},{9,10},{10,11},{11... | collective-permute-start | bytes 196616 | tf_op jit(solution)/shard_map/ppermute | solution.py:13
  29.3 95.5 %collective-permute-start.3 = (bf16[8,2048]{1,0:T(8,128)(2,1)S(1)}, bf16[8,2048]{1,0:T(8,128)(2,1)S(1)}, u32[]{:S(2)}, u32[]{:S(2)}) collective-permute-start(bf16[8,2048]{1,0:T(8,128)(2,1)S(1)} %get-tuple-element.12), channel_id=1, source_target_pairs={{1,0},{2,1},{3,2},{4,3},{5,4},{6,5},{7,6},{9,8},{10,9},{11,10},{12... | collective-permute-start | bytes 98312 | tf_op jit(solution)/shard_map/ppermute | solution.py:14
  31.3 93.6 %collective-permute-start.2 = (bf16[8,2048]{1,0:T(8,128)(2,1)S(1)}, bf16[8,2048]{1,0:T(8,128)(2,1)S(1)}, u32[]{:S(2)}, u32[]{:S(2)}) collective-permute-start(bf16[8,2048]{1,0:T(8,128)(2,1)S(1)} %get-tuple-element.11), channel_id=1, source_target_pairs={{0,1},{1,2},{2,3},{3,4},{4,5},{5,6},{6,7},{8,9},{9,10},{10,11},{11... | collective-permute-start | bytes 98312 | tf_op jit(solution)/shard_map/ppermute | solution.py:13
  126.2 5.2 %slice-start = ((s8[8388608]{0:T(1024)(128)(4,1)}), s8[4194304]{0:T(1024)(128)(4,1)S(1)}, s32[]{:S(2)}) async-start(s8[8388608]{0:T(1024)(128)(4,1)} %bitcast.42), calls=%async_computation.6 | async-start | bytes 8388608
  126.2 6.0 %slice-start.1 = ((s8[8388608]{0:T(1024)(128)(4,1)}), s8[4194304]{0:T(1024)(128)(4,1)S(1)}, s32[]{:S(2)}) async-start(s8[8388608]{0:T(1024)(128)(4,1)} %bitcast.42), calls=%async_computation.7 | async-start | bytes 8388608
  142.2 1.4 copy-start.1
  145.1 17.0 %all-to-all-start.1 = ((bf16[128,8,256]{2,0,1:T(8,128)(2,1)}), bf16[128,8,256]{2,0,1:T(8,128)(2,1)S(1)}, u32[]{:S(2)}, u32[]{:S(2)}) async-start(bf16[128,8,256]{2,0,1:T(8,128)(2,1)} %bitcast.40), calls=%async_computation.1 | async-start | bytes 1048576 | tf_op jit(solution)/shard_map/all_to_all | solution.py:44
  152.6 85.2 %reduce-scatter.2.cloned.1.call-start = ((), (), s32[]{:S(2)}) async-start(), calls=%async_computation.4 | async-start | bytes 2228224 | tf_op jit(solution)/shard_map/reduce_scatter | solution.py:48
Sparse Core Ops, SparseCore 0:
  29.4 110.1 all-gather.2
  167.0 70.7 reduce-scatter.1
